TPU v7x, 32 devices: a whole 2x2x4 slice. The times are simulated.
32 devices in a mesh: slab: 4 (over y, x), rcv: 8 (over z, core).
Axes of the slice: x: 2, y: 2, z: 4, core: 2. Of those that a mesh axis runs over, the one named last changes fastest.
Arguments:
- adjoint_now: float32 [8, 16, 128, 128], P('rcv', 'slab'), may hold values from -6 to 6
- adjoint_before: float32 [8, 16, 128, 128], P('rcv', 'slab'), may hold values from -6 to 6
- courant_field: float32 [16, 128, 128], P('slab'), may hold values from 0.04 to 0.2
- log_buoyancy: float32 [16, 128, 128], P('slab'), may hold values from -0.3 to 0.3
- snapshot_store: float32 [8, 16, 128, 128], P('rcv', 'slab'), may hold values from -6 to 6
- owner_order: int32 [8], replicated, may hold values from 0 to 7, each once
- receiver_cells: int32 [8], P('rcv'), may hold values from 0 to 262143
- receiver_traces: float32 [8, 8], P('rcv'), may hold values from -6 to 6
- residual_weights: float32 [8], P('rcv'), may hold values from -0.3 to 0.3
Outputs:
- sensitivity: float32 [16, 128, 128], P('slab', 'rcv')
- adjoint_after: float32 [8, 16, 128, 128], P('rcv', 'slab')
Inputs may be any that keep to these rules, and one draw needn't show every extreme that they name: Each slot number appears once; checkpoint k reads slot owner_order[k] for k < 4. `receiver_cells`: a cell of the grid.
All inputs are finite; a program needn't handle non-finite values.
Results may differ from a plain program's by a relative error of at most 0.0003.
Values sent between devices are 32-bit elements; how exact they have to be, the bound alone decides.
No kernel may reach another device: no remote copies, remote signals or barrier semaphores. Data moves between devices by JAX's collectives and lax.ppermute only.
A program may use at most 64 MiB of HBM per device.

v0:
```python
import jax
import jax.numpy as jnp
from jax import lax
from jax.sharding import PartitionSpec as P

SNAPS = 4


def extended(shard, sides, width):
    for axis, dim in sides:
        peers, length = (lax.axis_size(axis), shard.shape[dim])
        up = [(i, (i + 1) % peers) for i in range(peers - 1)]
        down = [(j, i) for i, j in up]
        last = lax.slice_in_dim(shard, length - width, length, axis=dim)
        leading = lax.slice_in_dim(shard, 0, width, axis=dim)
        before = lax.ppermute(last, axis, up)
        after = lax.ppermute(leading, axis, down)
        shard = jnp.concatenate([before, shard, after], axis=dim)
    return shard


def from_root(block, axis, owner):
    block = jnp.where(lax.axis_index(axis) == owner, block, jnp.zeros_like(block))
    return lax.psum(block, axis)


def piece_of(field, axis_no, begin, extent):
    return lax.slice_in_dim(field, begin, begin + extent, axis=axis_no)


def pad_axis(field, axis_no):
    widths = [(0, 0)] * field.ndim
    widths[axis_no] = (2, 2)
    return jnp.pad(field, widths)


def second_diff(field, axis_no, extent):
    outer = piece_of(field, axis_no, 0, extent) + piece_of(field, axis_no, 4, extent)
    inner = piece_of(field, axis_no, 1, extent) + piece_of(field, axis_no, 3, extent)
    return (16.0 * inner - outer - 30.0 * piece_of(field, axis_no, 2, extent)) / 12.0


def first_diff(field, axis_no, extent):
    inner = piece_of(field, axis_no, 3, extent) - piece_of(field, axis_no, 1, extent)
    outer = piece_of(field, axis_no, 4, extent) - piece_of(field, axis_no, 0, extent)
    return (8.0 * inner - outer) / 12.0


def slopes(log_ext):
    width = log_ext.shape[0] - 4
    centre = piece_of(log_ext, 0, 2, width)
    wide_y = pad_axis(centre, 1)
    wide_z = pad_axis(centre, 2)
    return jnp.stack(
        [
            first_diff(log_ext, 0, width),
            first_diff(wide_y, 1, centre.shape[1]),
            first_diff(wide_z, 2, centre.shape[2]),
        ]
    )


def advance(field, before, courant, gradient):
    first_axis = field.ndim - 3
    width = field.shape[first_axis] - 4
    centre = piece_of(field, first_axis, 2, width)
    wide_y = pad_axis(centre, first_axis + 1)
    wide_z = pad_axis(centre, first_axis + 2)
    size_y = field.shape[first_axis + 1]
    size_z = field.shape[first_axis + 2]
    curvature = (
        second_diff(field, first_axis, width)
        + second_diff(wide_y, first_axis + 1, size_y)
        + second_diff(wide_z, first_axis + 2, size_z)
    )
    drift_term = (
        gradient[0] * first_diff(field, first_axis, width)
        + gradient[1] * first_diff(wide_y, first_axis + 1, size_y)
        + gradient[2] * first_diff(wide_z, first_axis + 2, size_z)
    )
    return 2.0 * centre - before + courant * (curvature + drift_term)


def local(
    adjoint_now,
    adjoint_before,
    courant_field,
    log_buoyancy,
    snapshot_store,
    owner_order,
    receiver_cells,
    receiver_traces,
    residual_weights,
):
    slab_rows = courant_field.shape[0]
    size_y = courant_field.shape[1]
    size_z = courant_field.shape[2]
    row_anchor = lax.axis_index("slab") * slab_rows
    model_ext = extended(jnp.stack([courant_field, log_buoyancy]), (("slab", 1),), 4)
    courant_ext = model_ext[0, 2 : slab_rows + 6]
    gradient = slopes(model_ext[1])
    plane_ids = lax.broadcasted_iota(
        jnp.int32, (size_y, size_z), 0
    ) * size_z + lax.broadcasted_iota(jnp.int32, (size_y, size_z), 1)
    cell_column = receiver_cells[:, None, None, None]
    current = adjoint_now
    previous = adjoint_before
    kernel_sum = jnp.zeros((slab_rows, size_y, size_z), jnp.float32)
    for snap_index in range(SNAPS):
        forward_field = from_root(snapshot_store[0], "rcv", owner_order[snap_index])
        for half_step in range(2):
            widened = extended(current, (("slab", 1),), 2)
            upcoming = advance(
                widened,
                previous,
                courant_ext[4 - 2 : 4 - 2 + slab_rows],
                gradient[:, 4 - 2 : 4 - 2 + slab_rows],
            )
            global_rows = row_anchor - 4 + 4 + lax.broadcasted_iota(jnp.int32, (slab_rows,), 0)
            flat_ids = global_rows[:, None, None] * (size_y * size_z) + plane_ids[None]
            amplitude = receiver_traces[:, 2 * snap_index + half_step][:, None, None, None]
            upcoming = upcoming + jnp.where(flat_ids[None] == cell_column, amplitude, 0.0)
            previous = current
            current = upcoming
        kernel_terms = jnp.sum(
            residual_weights[:, None, None, None] * current * forward_field, axis=0
        )
        kernel_sum = kernel_sum + kernel_terms
    sensitivity = lax.psum_scatter(kernel_sum, "rcv", scatter_dimension=1, tiled=True)
    return (sensitivity, current)


def solution(mesh):
    placed = (
        P("rcv", "slab", None, None),
        P("rcv", "slab", None, None),
        P("slab", None, None),
        P("slab", None, None),
        P("rcv", "slab", None, None),
        P(),
        P("rcv"),
        P("rcv", None),
        P("rcv"),
    )
    return jax.shard_map(
        local,
        mesh=mesh,
        in_specs=placed,
        out_specs=(P("slab", "rcv", None), P("rcv", "slab", None, None)),
        check_vma=False,
    )
```

profile of v0, /device:TPU:0, one launch (start us, length us, event | category | flops | bytes accessed | tf_op | source)
XLA Modules:
  0.0 207.6 jit_solution(17127720802497031113)
XLA Ops:
  7.3 1.1 pad_maximum_fusion.1
  8.4 4.9 %collective-permute-start.2 = (f32[2,4,128,128]{3,2,1,0:T(8,128)S(1)}, f32[2,4,128,128]{3,2,1,0:T(8,128)S(1)}, u32[]{:S(2)}, u32[]{:S(2)}) collective-permute-start(f32[2,4,128,128]{3,2,1,0:T(8,128)S(1)} %pad_maximum_fusion.1), channel_id=1, source_target_pairs={{0,8},{8,16},{16,24},{1,9},{9,17},{17,25},{2,10},{10,18},{18,26},{... | collective-permute-start | bytes 1572872 | tf_op jit(solution)/shard_map/ppermute | solution.py:16
  13.3 1.3 collective-permute-start.3
  14.6 1.0 fusion.58
  15.6 4.6 %collective-permute-start = (f32[1,2,128,128]{3,2,1,0:T(8,128)S(1)}, f32[1,2,128,128]{3,2,1,0:T(8,128)S(1)}, u32[]{:S(2)}, u32[]{:S(2)}) collective-permute-start(f32[1,2,128,128]{3,2,1,0:T(8,128)S(1)} %get-tuple-element.31), channel_id=1, source_target_pairs={{0,8},{8,16},{16,24},{1,9},{9,17},{17,25},{2,10},{10,18},{18,26},{... | collective-permute-start | bytes 393224 | tf_op jit(solution)/shard_map/ppermute | solution.py:16
  20.1 1.3 collective-permute-start.1
  22.2 0.7 fusion.59
  22.9 4.4 %collective-permute-done = f32[1,2,128,128]{3,2,1,0:T(8,128)S(1)} collective-permute-done((f32[1,2,128,128]{3,2,1,0:T(8,128)S(1)}, f32[1,2,128,128]{3,2,1,0:T(8,128)S(1)}, u32[]{:S(2)}, u32[]{:S(2)}) %collective-permute-start) | collective-permute-done | bytes 131104 | tf_op jit(solution)/shard_map/ppermute | solution.py:16
  27.3 15.9 %collective-permute-done.1 = f32[1,2,128,128]{3,2,1,0:T(8,128)S(1)} collective-permute-done((f32[1,2,128,128]{3,2,1,0:T(8,128)S(1)}, f32[1,2,128,128]{3,2,1,0:T(8,128)S(1)}, u32[]{:S(2)}, u32[]{:S(2)}) %collective-permute-start.1) | collective-permute-done | bytes 131104 | tf_op jit(solution)/shard_map/ppermute | solution.py:17
  43.3 0.1 pad_maximum_fusion
  43.6 0.8 multiply_bitcast_fusion
  44.4 0.2 copy-done.3
  44.5 1.1 fusion.47
  45.7 3.4 %collective-permute-start.4 = (f32[1,2,128,128]{3,2,1,0:T(8,128)S(1)}, f32[1,2,128,128]{3,2,1,0:T(8,128)S(1)}, u32[]{:S(2)}, u32[]{:S(2)}) collective-permute-start(f32[1,2,128,128]{3,2,1,0:T(8,128)S(1)} %get-tuple-element.28), channel_id=1, source_target_pairs={{0,8},{8,16},{16,24},{1,9},{9,17},{17,25},{2,10},{10,18},{18,26},{... | collective-permute-start | bytes 393224 | tf_op jit(solution)/shard_map/ppermute | solution.py:16
  49.1 1.3 collective-permute-start.5
  50.4 1.2 collective-permute-done.4
  51.6 4.4 %collective-permute-done.5 = f32[1,2,128,128]{3,2,1,0:T(8,128)S(1)} collective-permute-done((f32[1,2,128,128]{3,2,1,0:T(8,128)S(1)}, f32[1,2,128,128]{3,2,1,0:T(8,128)S(1)}, u32[]{:S(2)}, u32[]{:S(2)}) %collective-permute-start.5) | collective-permute-done | bytes 131104 | tf_op jit(solution)/shard_map/ppermute | solution.py:17
  56.0 1.2 fusion.44
  57.2 2.8 %collective-permute-start.6 = (f32[1,2,128,128]{3,2,1,0:T(8,128)S(1)}, f32[1,2,128,128]{3,2,1,0:T(8,128)S(1)}, u32[]{:S(2)}, u32[]{:S(2)}) collective-permute-start(f32[1,2,128,128]{3,2,1,0:T(8,128)S(1)} %get-tuple-element.26), channel_id=1, source_target_pairs={{0,8},{8,16},{16,24},{1,9},{9,17},{17,25},{2,10},{10,18},{18,26},{... | collective-permute-start | bytes 393224 | tf_op jit(solution)/shard_map/ppermute | solution.py:16
  60.0 1.3 collective-permute-start.7
  61.3 1.2 collective-permute-done.6
  62.5 4.4 %collective-permute-done.7 = f32[1,2,128,128]{3,2,1,0:T(8,128)S(1)} collective-permute-done((f32[1,2,128,128]{3,2,1,0:T(8,128)S(1)}, f32[1,2,128,128]{3,2,1,0:T(8,128)S(1)}, u32[]{:S(2)}, u32[]{:S(2)}) %collective-permute-start.7) | collective-permute-done | bytes 131104 | tf_op jit(solution)/shard_map/ppermute | solution.py:17
  66.9 1.2 fusion.41
  68.1 2.8 %collective-permute-start.8 = (f32[1,2,128,128]{3,2,1,0:T(8,128)S(1)}, f32[1,2,128,128]{3,2,1,0:T(8,128)S(1)}, u32[]{:S(2)}, u32[]{:S(2)}) collective-permute-start(f32[1,2,128,128]{3,2,1,0:T(8,128)S(1)} %get-tuple-element.24), channel_id=1, source_target_pairs={{0,8},{8,16},{16,24},{1,9},{9,17},{17,25},{2,10},{10,18},{18,26},{... | collective-permute-start | bytes 393224 | tf_op jit(solution)/shard_map/ppermute | solution.py:16
  70.9 1.3 collective-permute-start.9
  72.2 1.2 collective-permute-done.8
  73.4 4.4 %collective-permute-done.9 = f32[1,2,128,128]{3,2,1,0:T(8,128)S(1)} collective-permute-done((f32[1,2,128,128]{3,2,1,0:T(8,128)S(1)}, f32[1,2,128,128]{3,2,1,0:T(8,128)S(1)}, u32[]{:S(2)}, u32[]{:S(2)}) %collective-permute-start.9) | collective-permute-done | bytes 131104 | tf_op jit(solution)/shard_map/ppermute | solution.py:17
  77.8 1.2 fusion.38
  79.0 3.0 %collective-permute-start.10 = (f32[1,2,128,128]{3,2,1,0:T(8,128)S(1)}, f32[1,2,128,128]{3,2,1,0:T(8,128)S(1)}, u32[]{:S(2)}, u32[]{:S(2)}) collective-permute-start(f32[1,2,128,128]{3,2,1,0:T(8,128)S(1)} %get-tuple-element.22), channel_id=1, source_target_pairs={{0,8},{8,16},{16,24},{1,9},{9,17},{17,25},{2,10},{10,18},{18,26},{... | collective-permute-start | bytes 393224 | tf_op jit(solution)/shard_map/ppermute | solution.py:16
  82.0 1.3 collective-permute-start.11
  83.3 1.2 collective-permute-done.10
  84.5 4.4 %collective-permute-done.11 = f32[1,2,128,128]{3,2,1,0:T(8,128)S(1)} collective-permute-done((f32[1,2,128,128]{3,2,1,0:T(8,128)S(1)}, f32[1,2,128,128]{3,2,1,0:T(8,128)S(1)}, u32[]{:S(2)}, u32[]{:S(2)}) %collective-permute-start.11) | collective-permute-done | bytes 131104 | tf_op jit(solution)/shard_map/ppermute | solution.py:17
  88.9 1.2 fusion.35
  90.1 3.0 %collective-permute-start.12 = (f32[1,2,128,128]{3,2,1,0:T(8,128)S(1)}, f32[1,2,128,128]{3,2,1,0:T(8,128)S(1)}, u32[]{:S(2)}, u32[]{:S(2)}) collective-permute-start(f32[1,2,128,128]{3,2,1,0:T(8,128)S(1)} %get-tuple-element.20), channel_id=1, source_target_pairs={{0,8},{8,16},{16,24},{1,9},{9,17},{17,25},{2,10},{10,18},{18,26},{... | collective-permute-start | bytes 393224 | tf_op jit(solution)/shard_map/ppermute | solution.py:16
  93.1 1.3 collective-permute-start.13
  94.4 0.7 fusion.60
  97.7 2.3 %collective-permute-done.13 = f32[1,2,128,128]{3,2,1,0:T(8,128)S(1)} collective-permute-done((f32[1,2,128,128]{3,2,1,0:T(8,128)S(1)}, f32[1,2,128,128]{3,2,1,0:T(8,128)S(1)}, u32[]{:S(2)}, u32[]{:S(2)}) %collective-permute-start.13) | collective-permute-done | bytes 131104 | tf_op jit(solution)/shard_map/ppermute | solution.py:17
  100.0 1.2 fusion.32
  101.2 2.9 %collective-permute-start.14 = (f32[1,2,128,128]{3,2,1,0:T(8,128)S(1)}, f32[1,2,128,128]{3,2,1,0:T(8,128)S(1)}, u32[]{:S(2)}, u32[]{:S(2)}) collective-permute-start(f32[1,2,128,128]{3,2,1,0:T(8,128)S(1)} %get-tuple-element.18), channel_id=1, source_target_pairs={{0,8},{8,16},{16,24},{1,9},{9,17},{17,25},{2,10},{10,18},{18,26},{... | collective-permute-start | bytes 393224 | tf_op jit(solution)/shard_map/ppermute | solution.py:16
  104.1 1.3 collective-permute-start.15
  105.4 1.0 broadcast_select_fusion.3
  106.6 4.4 %collective-permute-done.15 = f32[1,2,128,128]{3,2,1,0:T(8,128)S(1)} collective-permute-done((f32[1,2,128,128]{3,2,1,0:T(8,128)S(1)}, f32[1,2,128,128]{3,2,1,0:T(8,128)S(1)}, u32[]{:S(2)}, u32[]{:S(2)}) %collective-permute-start.15) | collective-permute-done | bytes 131104 | tf_op jit(solution)/shard_map/ppermute | solution.py:17
  111.0 1.1 fusion.29
  112.1 4.1 %collective-permute-start.16 = (f32[1,2,128,128]{3,2,1,0:T(8,128)S(1)}, f32[1,2,128,128]{3,2,1,0:T(8,128)S(1)}, u32[]{:S(2)}, u32[]{:S(2)}) collective-permute-start(f32[1,2,128,128]{3,2,1,0:T(8,128)S(1)} %get-tuple-element.15), channel_id=1, source_target_pairs={{0,8},{8,16},{16,24},{1,9},{9,17},{17,25},{2,10},{10,18},{18,26},{... | collective-permute-start | bytes 393224 | tf_op jit(solution)/shard_map/ppermute | solution.py:16
  116.2 1.3 collective-permute-start.17
  118.2 49.3 %all-reduce.21.cloned.1.call-done = (f32[1,4,128,128]{3,2,1,0:T(8,128)}, f32[1,4,128,128]{3,2,1,0:T(8,128)}, f32[1,4,128,128]{3,2,1,0:T(8,128)}, f32[1,4,128,128]{3,2,1,0:T(8,128)}) async-done(((f32[1,4,128,128]{3,2,1,0:T(8,128)}, f32[1,4,128,128]{3,2,1,0:T(8,128)}, f32[1,4,128,128]{3,2,1,0:T(8,128)}, f32[1,4,128,128]{3,2,1,0:T(8,128)}), (f32[1,4,128,128]{3,2,1,0:T(8,128)}, f32[1,4,128,128]{3,2,1,0:T(8,128)}, ...) | async-done | bytes 1048592 | tf_op jit(solution)/shard_map/psum | solution.py:24
  167.4 3.2 %add_bitcast_fusion = (f32[4,128,128]{2,1,0:T(8,128)}, f32[1,4,128,128]{3,2,1,0:T(8,128)}) fusion(f32[1,4,128,128]{3,2,1,0:T(8,128)} %get-tuple-element.2, f32[1,4,128,128]{3,2,1,0:T(8,128)} %get-tuple-element.3, f32[1,4,128,128]{3,2,1,0:T(8,128)S(1)} %fusion.32, f32[1,4,128,128]{3,2,1,0:T(8,128)} %get-tuple-element.4, f32[1,4,128,128]{3,2,1,0:T(8,128)S(1)} %fusion.38, ...), kind=kLoop, calls=%fused_computation.144 | loop fusion | flops 4128768 | bytes 3997724 | tf_op jit(solution)/shard_map/add | solution.py:128
  170.7 30.1 %reduce-scatter.2.cloned.1.call-done = f32[4,16,128]{2,1,0:T(8,128)} async-done(((f32[4,128,128]{2,1,0:T(8,128)}), f32[4,16,128]{2,1,0:T(8,128)}) %reduce-scatter.2.cloned.1.call-update) | async-done | bytes 32784 | tf_op jit(solution)/shard_map/reduce_scatter | solution.py:129
  (37 shorter events, 0.7 us)
Async XLA Ops:
  7.2 36.1 %copy-start = (f32[4,128,128]{2,1,0:T(8,128)S(1)}, f32[4,128,128]{2,1,0:T(8,128)}, u32[]{:S(2)}) copy-start(f32[4,128,128]{2,1,0:T(8,128)} %param.11) | copy-start | bytes 786436
  7.2 36.1 %copy-start.2 = (f32[4,128,128]{2,1,0:T(8,128)S(1)}, f32[4,128,128]{2,1,0:T(8,128)}, u32[]{:S(2)}) copy-start(f32[4,128,128]{2,1,0:T(8,128)} %param.12) | copy-start | bytes 786436
  7.2 20.1 %copy-start.1 = (f32[1,4,128,128]{3,2,1,0:T(8,128)S(1)}, f32[1,4,128,128]{3,2,1,0:T(8,128)}, u32[]{:S(2)}) copy-start(f32[1,4,128,128]{3,2,1,0:T(8,128)} %param.9) | copy-start | bytes 786436
  7.2 15.0 %copy-start.5 = (f32[1,8]{1,0:T(1,128)S(1)}, f32[1,8]{1,0:T(1,128)}, u32[]{:S(2)}) copy-start(f32[1,8]{1,0:T(1,128)} %param.16) | copy-start | bytes 100
  7.2 160.2 %all-reduce.21.cloned.1.call-start = ((), (), s32[]{:S(2)}) async-start(), calls=%async_computation.2 | async-start | bytes 2097152 | tf_op jit(solution)/shard_map/psum | solution.py:24
  8.4 34.9 %collective-permute-start.2 = (f32[2,4,128,128]{3,2,1,0:T(8,128)S(1)}, f32[2,4,128,128]{3,2,1,0:T(8,128)S(1)}, u32[]{:S(2)}, u32[]{:S(2)}) collective-permute-start(f32[2,4,128,128]{3,2,1,0:T(8,128)S(1)} %pad_maximum_fusion.1), channel_id=1, source_target_pairs={{0,8},{8,16},{16,24},{1,9},{9,17},{17,25},{2,10},{10,18},{18,26},{... | collective-permute-start | bytes 1572872 | tf_op jit(solution)/shard_map/ppermute | solution.py:16
  13.3 30.0 %collective-permute-start.3 = (f32[2,4,128,128]{3,2,1,0:T(8,128)S(1)}, f32[2,4,128,128]{3,2,1,0:T(8,128)S(1)}, u32[]{:S(2)}, u32[]{:S(2)}) collective-permute-start(f32[2,4,128,128]{3,2,1,0:T(8,128)S(1)} %pad_maximum_fusion.1), channel_id=1, source_target_pairs={{8,0},{16,8},{24,16},{9,1},{17,9},{25,17},{10,2},{18,10},{26,18},{... | collective-permute-start | bytes 1572872 | tf_op jit(solution)/shard_map/ppermute | solution.py:17
  15.6 11.6 %collective-permute-start = (f32[1,2,128,128]{3,2,1,0:T(8,128)S(1)}, f32[1,2,128,128]{3,2,1,0:T(8,128)S(1)}, u32[]{:S(2)}, u32[]{:S(2)}) collective-permute-start(f32[1,2,128,128]{3,2,1,0:T(8,128)S(1)} %get-tuple-element.31), channel_id=1, source_target_pairs={{0,8},{8,16},{16,24},{1,9},{9,17},{17,25},{2,10},{10,18},{18,26},{... | collective-permute-start | bytes 393224 | tf_op jit(solution)/shard_map/ppermute | solution.py:16
  20.1 23.1 %collective-permute-start.1 = (f32[1,2,128,128]{3,2,1,0:T(8,128)S(1)}, f32[1,2,128,128]{3,2,1,0:T(8,128)S(1)}, u32[]{:S(2)}, u32[]{:S(2)}) collective-permute-start(f32[1,2,128,128]{3,2,1,0:T(8,128)S(1)} %get-tuple-element.32), channel_id=1, source_target_pairs={{8,0},{16,8},{24,16},{9,1},{17,9},{25,17},{10,2},{18,10},{26,18},{... | collective-permute-start | bytes 393224 | tf_op jit(solution)/shard_map/ppermute | solution.py:17
  43.6 1.0 copy-start.3
  45.7 5.9 %collective-permute-start.4 = (f32[1,2,128,128]{3,2,1,0:T(8,128)S(1)}, f32[1,2,128,128]{3,2,1,0:T(8,128)S(1)}, u32[]{:S(2)}, u32[]{:S(2)}) collective-permute-start(f32[1,2,128,128]{3,2,1,0:T(8,128)S(1)} %get-tuple-element.28), channel_id=1, source_target_pairs={{0,8},{8,16},{16,24},{1,9},{9,17},{17,25},{2,10},{10,18},{18,26},{... | collective-permute-start | bytes 393224 | tf_op jit(solution)/shard_map/ppermute | solution.py:16
  49.1 6.9 %collective-permute-start.5 = (f32[1,2,128,128]{3,2,1,0:T(8,128)S(1)}, f32[1,2,128,128]{3,2,1,0:T(8,128)S(1)}, u32[]{:S(2)}, u32[]{:S(2)}) collective-permute-start(f32[1,2,128,128]{3,2,1,0:T(8,128)S(1)} %get-tuple-element.27), channel_id=1, source_target_pairs={{8,0},{16,8},{24,16},{9,1},{17,9},{25,17},{10,2},{18,10},{26,18},{... | collective-permute-start | bytes 393224 | tf_op jit(solution)/shard_map/ppermute | solution.py:17
  57.2 5.3 %collective-permute-start.6 = (f32[1,2,128,128]{3,2,1,0:T(8,128)S(1)}, f32[1,2,128,128]{3,2,1,0:T(8,128)S(1)}, u32[]{:S(2)}, u32[]{:S(2)}) collective-permute-start(f32[1,2,128,128]{3,2,1,0:T(8,128)S(1)} %get-tuple-element.26), channel_id=1, source_target_pairs={{0,8},{8,16},{16,24},{1,9},{9,17},{17,25},{2,10},{10,18},{18,26},{... | collective-permute-start | bytes 393224 | tf_op jit(solution)/shard_map/ppermute | solution.py:16
  60.0 6.9 %collective-permute-start.7 = (f32[1,2,128,128]{3,2,1,0:T(8,128)S(1)}, f32[1,2,128,128]{3,2,1,0:T(8,128)S(1)}, u32[]{:S(2)}, u32[]{:S(2)}) collective-permute-start(f32[1,2,128,128]{3,2,1,0:T(8,128)S(1)} %get-tuple-element.25), channel_id=1, source_target_pairs={{8,0},{16,8},{24,16},{9,1},{17,9},{25,17},{10,2},{18,10},{26,18},{... | collective-permute-start | bytes 393224 | tf_op jit(solution)/shard_map/ppermute | solution.py:17
  68.1 5.3 %collective-permute-start.8 = (f32[1,2,128,128]{3,2,1,0:T(8,128)S(1)}, f32[1,2,128,128]{3,2,1,0:T(8,128)S(1)}, u32[]{:S(2)}, u32[]{:S(2)}) collective-permute-start(f32[1,2,128,128]{3,2,1,0:T(8,128)S(1)} %get-tuple-element.24), channel_id=1, source_target_pairs={{0,8},{8,16},{16,24},{1,9},{9,17},{17,25},{2,10},{10,18},{18,26},{... | collective-permute-start | bytes 393224 | tf_op jit(solution)/shard_map/ppermute | solution.py:16
  70.9 6.9 %collective-permute-start.9 = (f32[1,2,128,128]{3,2,1,0:T(8,128)S(1)}, f32[1,2,128,128]{3,2,1,0:T(8,128)S(1)}, u32[]{:S(2)}, u32[]{:S(2)}) collective-permute-start(f32[1,2,128,128]{3,2,1,0:T(8,128)S(1)} %get-tuple-element.23), channel_id=1, source_target_pairs={{8,0},{16,8},{24,16},{9,1},{17,9},{25,17},{10,2},{18,10},{26,18},{... | collective-permute-start | bytes 393224 | tf_op jit(solution)/shard_map/ppermute | solution.py:17
  79.0 15.5 %copy-start.6 = (s32[8]{0:T(128)S(1)}, s32[8]{0:T(128)}, u32[]{:S(2)}) copy-start(s32[8]{0:T(128)} %param.14) | copy-start | bytes 100
  79.0 5.5 %collective-permute-start.10 = (f32[1,2,128,128]{3,2,1,0:T(8,128)S(1)}, f32[1,2,128,128]{3,2,1,0:T(8,128)S(1)}, u32[]{:S(2)}, u32[]{:S(2)}) collective-permute-start(f32[1,2,128,128]{3,2,1,0:T(8,128)S(1)} %get-tuple-element.22), channel_id=1, source_target_pairs={{0,8},{8,16},{16,24},{1,9},{9,17},{17,25},{2,10},{10,18},{18,26},{... | collective-permute-start | bytes 393224 | tf_op jit(solution)/shard_map/ppermute | solution.py:16
  82.0 6.9 %collective-permute-start.11 = (f32[1,2,128,128]{3,2,1,0:T(8,128)S(1)}, f32[1,2,128,128]{3,2,1,0:T(8,128)S(1)}, u32[]{:S(2)}, u32[]{:S(2)}) collective-permute-start(f32[1,2,128,128]{3,2,1,0:T(8,128)S(1)} %get-tuple-element.21), channel_id=1, source_target_pairs={{8,0},{16,8},{24,16},{9,1},{17,9},{25,17},{10,2},{18,10},{26,18},{... | collective-permute-start | bytes 393224 | tf_op jit(solution)/shard_map/ppermute | solution.py:17
  90.1 15.3 %copy-start.4 = (f32[1,4,128,128]{3,2,1,0:T(8,128)S(1)}, f32[1,4,128,128]{3,2,1,0:T(8,128)}, u32[]{:S(2)}) copy-start(f32[1,4,128,128]{3,2,1,0:T(8,128)} %param.13) | copy-start | bytes 786436
  90.1 7.6 %collective-permute-start.12 = (f32[1,2,128,128]{3,2,1,0:T(8,128)S(1)}, f32[1,2,128,128]{3,2,1,0:T(8,128)S(1)}, u32[]{:S(2)}, u32[]{:S(2)}) collective-permute-start(f32[1,2,128,128]{3,2,1,0:T(8,128)S(1)} %get-tuple-element.20), channel_id=1, source_target_pairs={{0,8},{8,16},{16,24},{1,9},{9,17},{17,25},{2,10},{10,18},{18,26},{... | collective-permute-start | bytes 393224 | tf_op jit(solution)/shard_map/ppermute | solution.py:16
  93.1 6.9 %collective-permute-start.13 = (f32[1,2,128,128]{3,2,1,0:T(8,128)S(1)}, f32[1,2,128,128]{3,2,1,0:T(8,128)S(1)}, u32[]{:S(2)}, u32[]{:S(2)}) collective-permute-start(f32[1,2,128,128]{3,2,1,0:T(8,128)S(1)} %get-tuple-element.19), channel_id=1, source_target_pairs={{8,0},{16,8},{24,16},{9,1},{17,9},{25,17},{10,2},{18,10},{26,18},{... | collective-permute-start | bytes 393224 | tf_op jit(solution)/shard_map/ppermute | solution.py:17
  101.2 5.4 %collective-permute-start.14 = (f32[1,2,128,128]{3,2,1,0:T(8,128)S(1)}, f32[1,2,128,128]{3,2,1,0:T(8,128)S(1)}, u32[]{:S(2)}, u32[]{:S(2)}) collective-permute-start(f32[1,2,128,128]{3,2,1,0:T(8,128)S(1)} %get-tuple-element.18), channel_id=1, source_target_pairs={{0,8},{8,16},{16,24},{1,9},{9,17},{17,25},{2,10},{10,18},{18,26},{... | collective-permute-start | bytes 393224 | tf_op jit(solution)/shard_map/ppermute | solution.py:16
  104.1 6.9 %collective-permute-start.15 = (f32[1,2,128,128]{3,2,1,0:T(8,128)S(1)}, f32[1,2,128,128]{3,2,1,0:T(8,128)S(1)}, u32[]{:S(2)}, u32[]{:S(2)}) collective-permute-start(f32[1,2,128,128]{3,2,1,0:T(8,128)S(1)} %get-tuple-element.17), channel_id=1, source_target_pairs={{8,0},{16,8},{24,16},{9,1},{17,9},{25,17},{10,2},{18,10},{26,18},{... | collective-permute-start | bytes 393224 | tf_op jit(solution)/shard_map/ppermute | solution.py:17
  106.4 94.3 %reduce-scatter.2.cloned.1.call-start = ((), (), s32[]{:S(2)}) async-start(), calls=%async_computation.1 | async-start | bytes 294912 | tf_op jit(solution)/shard_map/reduce_scatter | solution.py:129
  112.1 55.3 %collective-permute-start.16 = (f32[1,2,128,128]{3,2,1,0:T(8,128)S(1)}, f32[1,2,128,128]{3,2,1,0:T(8,128)S(1)}, u32[]{:S(2)}, u32[]{:S(2)}) collective-permute-start(f32[1,2,128,128]{3,2,1,0:T(8,128)S(1)} %get-tuple-element.15), channel_id=1, source_target_pairs={{0,8},{8,16},{16,24},{1,9},{9,17},{17,25},{2,10},{10,18},{18,26},{... | collective-permute-start | bytes 393224 | tf_op jit(solution)/shard_map/ppermute | solution.py:16
  116.2 51.2 %collective-permute-start.17 = (f32[1,2,128,128]{3,2,1,0:T(8,128)S(1)}, f32[1,2,128,128]{3,2,1,0:T(8,128)S(1)}, u32[]{:S(2)}, u32[]{:S(2)}) collective-permute-start(f32[1,2,128,128]{3,2,1,0:T(8,128)S(1)} %get-tuple-element.16), channel_id=1, source_target_pairs={{8,0},{16,8},{24,16},{9,1},{17,9},{25,17},{10,2},{18,10},{26,18},{... | collective-permute-start | bytes 393224 | tf_op jit(solution)/shard_map/ppermute | solution.py:17
Sparse Core Ops, SparseCore 0:
  106.5 60.8 all-reduce.20
  170.8 29.9 reduce-scatter.1
where the time goes:
time: 208 us
  waiting for transfers between devices  129 us (62%)
  starting transfers between devices  43.3 us (21%)
  between operations  18.4 us (9%)
  other arithmetic  14.4 us (7%)
  local copies, waits for them, and re-layouts  2.83 us (1%)
    psum x1, waiting for transfers between devices, from_root(): return lax.psum(block, axis)  49.3 us
    ppermute x9, waiting for transfers between devices, extended(): after = lax.ppermute(leading, axis, down)  40 us
    ppermute x9, starting transfers between devices, extended(): before = lax.ppermute(last, axis, up)  31.6 us
    reduce_scatter x1, waiting for transfers between devices, local(): lax.psum_scatter(kernel_sum, 'rcv', scatter_dimension=1, tiled=True)  30.1 us
    ppermute x9, starting transfers between devices, extended(): after = lax.ppermute(leading, axis, down)  11.6 us
    ppermute x9, waiting for transfers between devices, extended(): before = lax.ppermute(last, axis, up)  9.28 us
    add x7, other arithmetic, local(): upcoming + jnp.where(flat_ids[None] == cell_column, amplitude, 0.0)  8.12 us
  transfers between devices with their start and end apart: 20, of which 15 were waited for; matrix products, arithmetic and copies ran while one was open for 2% of the time, Pallas kernels for 0%

commit v1 on v0

--- a/solution.py
+++ b/solution.py
@@ -21,7 +21,7 @@
 
 def from_root(block, axis, owner):
     block = jnp.where(lax.axis_index(axis) == owner, block, jnp.zeros_like(block))
-    return lax.psum(block, axis)
+    return jnp.sum(lax.all_gather(block, axis), axis=0)
 
 
 def piece_of(field, axis_no, begin, extent):

time: 208 us -> 179 us (0.86)
  waiting for transfers between devices: 129 us -> 91.9 us
  other arithmetic: 14.4 us -> 22 us
    psum x1 -> x0, waiting for transfers between devices: 49.3 us -> none  [from_root(): return lax.psum(block, axis)]
    reduce_sum x0 -> x4, other arithmetic: none -> 7.66 us  [from_root(): return jnp.sum(lax.all_gather(block, axis), axis=0)]
    all_gather x0 -> x4, waiting for transfers between devices: none -> 5.64 us  [from_root(): return jnp.sum(lax.all_gather(block, axis), axis=0)]
    ppermute x9, waiting for transfers between devices: 9.28 us -> 12.4 us  [extended(): before = lax.ppermute(last, axis, up)]
    ppermute x9, waiting for transfers between devices: 40 us -> 42.1 us  [extended(): after = lax.ppermute(leading, axis, down)]
  transfers between devices with their start and end apart: 20 -> 23, of which waited for: 15 -> 16; matrix products, arithmetic and copies ran while one was open for 2% -> 10% of each run, Pallas kernels for 0% -> 0%
where the time goes in v1:
time: 179 us; the launch traced here: 178 us
  waiting for transfers between devices  91.9 us (51%)
  starting transfers between devices  42.8 us (24%)
  other arithmetic  22 us (12%)
  between operations  18 us (10%)
  local copies, waits for them, and re-layouts  3.36 us (2%)
    ppermute x9, waiting for transfers between devices, extended(): after = lax.ppermute(leading, axis, down)  42.1 us
    ppermute x9, starting transfers between devices, extended(): before = lax.ppermute(last, axis, up)  31 us
    reduce_scatter x1, waiting for transfers between devices, local(): lax.psum_scatter(kernel_sum, 'rcv', scatter_dimension=1, tiled=True)  30.3 us
    ppermute x9, waiting for transfers between devices, extended(): before = lax.ppermute(last, axis, up)  12.4 us
    ppermute x9, starting transfers between devices, extended(): after = lax.ppermute(leading, axis, down)  11.6 us
    add x7, other arithmetic, local(): upcoming + jnp.where(flat_ids[None] == cell_column, amplitude, 0.0)  8.23 us
    reduce_sum x4, other arithmetic, from_root(): return jnp.sum(lax.all_gather(block, axis), axis=0)  7.66 us
    all_gather x4, waiting for transfers between devices, from_root(): return jnp.sum(lax.all_gather(block, axis), axis=0)  5.64 us
  transfers between devices with their start and end apart: 23, of which 16 were waited for; matrix products, arithmetic and copies ran while one was open for 10% of the time, Pallas kernels for 0%

profile of v1, /device:TPU:0, one launch (start us, length us, event | category | flops | bytes accessed | tf_op | source)
XLA Modules:
  0.0 178.1 jit_solution(10203318429118798044)
XLA Ops:
  7.2 1.4 fusion.64
  11.2 2.0 %broadcast_select_fusion.3 = (f32[1,4,128,128]{3,2,1,0:T(8,128)}, f32[1,4,128,128]{3,2,1,0:T(8,128)}, f32[1,4,128,128]{3,2,1,0:T(8,128)}, f32[1,4,128,128]{3,2,1,0:T(8,128)}) fusion(f32[1,4,128,128]{3,2,1,0:T(8,128)} %param.13, pred[]{:T(512)S(6)} %eq.89, pred[]{:T(512)S(6)} %eq.90, pred[]{:T(512)S(6)} %eq.92, pred[]{:T(512)S(6)} %eq.91), kind=kLoop, calls=%fused_computation.164 | loop fusion | flops 262144 | bytes 1310724 | tf_op jit(solution)/shard_map/jit(_where)/select_n | solution.py:23
  14.9 4.9 %collective-permute-start.2 = (f32[2,4,128,128]{3,2,1,0:T(8,128)S(1)}, f32[2,4,128,128]{3,2,1,0:T(8,128)S(1)}, u32[]{:S(2)}, u32[]{:S(2)}) collective-permute-start(f32[2,4,128,128]{3,2,1,0:T(8,128)S(1)} %pad_maximum_fusion.1), channel_id=1, source_target_pairs={{0,8},{8,16},{16,24},{1,9},{9,17},{17,25},{2,10},{10,18},{18,26},{... | collective-permute-start | bytes 1572872 | tf_op jit(solution)/shard_map/ppermute | solution.py:16
  19.8 1.3 collective-permute-start.3
  21.1 4.6 %collective-permute-start = (f32[1,2,128,128]{3,2,1,0:T(8,128)S(1)}, f32[1,2,128,128]{3,2,1,0:T(8,128)S(1)}, u32[]{:S(2)}, u32[]{:S(2)}) collective-permute-start(f32[1,2,128,128]{3,2,1,0:T(8,128)S(1)} %get-tuple-element.27), channel_id=1, source_target_pairs={{0,8},{8,16},{16,24},{1,9},{9,17},{17,25},{2,10},{10,18},{18,26},{... | collective-permute-start | bytes 393224 | tf_op jit(solution)/shard_map/ppermute | solution.py:16
  25.7 1.3 collective-permute-start.1
  28.4 5.3 %collective-permute-done = f32[1,2,128,128]{3,2,1,0:T(8,128)S(1)} collective-permute-done((f32[1,2,128,128]{3,2,1,0:T(8,128)S(1)}, f32[1,2,128,128]{3,2,1,0:T(8,128)S(1)}, u32[]{:S(2)}, u32[]{:S(2)}) %collective-permute-start) | collective-permute-done | bytes 131104 | tf_op jit(solution)/shard_map/ppermute | solution.py:16
  33.8 15.9 %collective-permute-done.1 = f32[1,2,128,128]{3,2,1,0:T(8,128)S(1)} collective-permute-done((f32[1,2,128,128]{3,2,1,0:T(8,128)S(1)}, f32[1,2,128,128]{3,2,1,0:T(8,128)S(1)}, u32[]{:S(2)}, u32[]{:S(2)}) %collective-permute-start.1) | collective-permute-done | bytes 131104 | tf_op jit(solution)/shard_map/ppermute | solution.py:17
  51.0 1.3 fusion.51
  52.3 3.4 %collective-permute-start.4 = (f32[1,2,128,128]{3,2,1,0:T(8,128)S(1)}, f32[1,2,128,128]{3,2,1,0:T(8,128)S(1)}, u32[]{:S(2)}, u32[]{:S(2)}) collective-permute-start(f32[1,2,128,128]{3,2,1,0:T(8,128)S(1)} %get-tuple-element.24), channel_id=1, source_target_pairs={{0,8},{8,16},{16,24},{1,9},{9,17},{17,25},{2,10},{10,18},{18,26},{... | collective-permute-start | bytes 393224 | tf_op jit(solution)/shard_map/ppermute | solution.py:16
  55.7 1.3 collective-permute-start.5
  57.1 1.1 collective-permute-done.4
  58.2 4.4 %collective-permute-done.5 = f32[1,2,128,128]{3,2,1,0:T(8,128)S(1)} collective-permute-done((f32[1,2,128,128]{3,2,1,0:T(8,128)S(1)}, f32[1,2,128,128]{3,2,1,0:T(8,128)S(1)}, u32[]{:S(2)}, u32[]{:S(2)}) %collective-permute-start.5) | collective-permute-done | bytes 131104 | tf_op jit(solution)/shard_map/ppermute | solution.py:17
  62.5 1.1 fusion.48
  63.7 2.8 %collective-permute-start.6 = (f32[1,2,128,128]{3,2,1,0:T(8,128)S(1)}, f32[1,2,128,128]{3,2,1,0:T(8,128)S(1)}, u32[]{:S(2)}, u32[]{:S(2)}) collective-permute-start(f32[1,2,128,128]{3,2,1,0:T(8,128)S(1)} %get-tuple-element.22), channel_id=1, source_target_pairs={{0,8},{8,16},{16,24},{1,9},{9,17},{17,25},{2,10},{10,18},{18,26},{... | collective-permute-start | bytes 393224 | tf_op jit(solution)/shard_map/ppermute | solution.py:16
  66.5 1.3 collective-permute-start.7
  67.8 1.2 collective-permute-done.6
  69.0 4.4 %collective-permute-done.7 = f32[1,2,128,128]{3,2,1,0:T(8,128)S(1)} collective-permute-done((f32[1,2,128,128]{3,2,1,0:T(8,128)S(1)}, f32[1,2,128,128]{3,2,1,0:T(8,128)S(1)}, u32[]{:S(2)}, u32[]{:S(2)}) %collective-permute-start.7) | collective-permute-done | bytes 131104 | tf_op jit(solution)/shard_map/ppermute | solution.py:17
  73.4 1.2 fusion.45
  74.6 2.8 %collective-permute-start.8 = (f32[1,2,128,128]{3,2,1,0:T(8,128)S(1)}, f32[1,2,128,128]{3,2,1,0:T(8,128)S(1)}, u32[]{:S(2)}, u32[]{:S(2)}) collective-permute-start(f32[1,2,128,128]{3,2,1,0:T(8,128)S(1)} %get-tuple-element.20), channel_id=1, source_target_pairs={{0,8},{8,16},{16,24},{1,9},{9,17},{17,25},{2,10},{10,18},{18,26},{... | collective-permute-start | bytes 393224 | tf_op jit(solution)/shard_map/ppermute | solution.py:16
  77.5 1.3 collective-permute-start.9
  78.8 1.2 collective-permute-done.8
  80.0 4.4 %collective-permute-done.9 = f32[1,2,128,128]{3,2,1,0:T(8,128)S(1)} collective-permute-done((f32[1,2,128,128]{3,2,1,0:T(8,128)S(1)}, f32[1,2,128,128]{3,2,1,0:T(8,128)S(1)}, u32[]{:S(2)}, u32[]{:S(2)}) %collective-permute-start.9) | collective-permute-done | bytes 131104 | tf_op jit(solution)/shard_map/ppermute | solution.py:17
  84.3 1.2 fusion.42
  85.5 2.8 %collective-permute-start.10 = (f32[1,2,128,128]{3,2,1,0:T(8,128)S(1)}, f32[1,2,128,128]{3,2,1,0:T(8,128)S(1)}, u32[]{:S(2)}, u32[]{:S(2)}) collective-permute-start(f32[1,2,128,128]{3,2,1,0:T(8,128)S(1)} %get-tuple-element.18), channel_id=1, source_target_pairs={{0,8},{8,16},{16,24},{1,9},{9,17},{17,25},{2,10},{10,18},{18,26},{... | collective-permute-start | bytes 393224 | tf_op jit(solution)/shard_map/ppermute | solution.py:16
  88.3 1.3 collective-permute-start.11
  89.6 1.2 collective-permute-done.10
  90.8 4.4 %collective-permute-done.11 = f32[1,2,128,128]{3,2,1,0:T(8,128)S(1)} collective-permute-done((f32[1,2,128,128]{3,2,1,0:T(8,128)S(1)}, f32[1,2,128,128]{3,2,1,0:T(8,128)S(1)}, u32[]{:S(2)}, u32[]{:S(2)}) %collective-permute-start.11) | collective-permute-done | bytes 131104 | tf_op jit(solution)/shard_map/ppermute | solution.py:17
  95.2 1.2 fusion.39
  96.4 3.1 %collective-permute-start.12 = (f32[1,2,128,128]{3,2,1,0:T(8,128)S(1)}, f32[1,2,128,128]{3,2,1,0:T(8,128)S(1)}, u32[]{:S(2)}, u32[]{:S(2)}) collective-permute-start(f32[1,2,128,128]{3,2,1,0:T(8,128)S(1)} %get-tuple-element.16), channel_id=1, source_target_pairs={{0,8},{8,16},{16,24},{1,9},{9,17},{17,25},{2,10},{10,18},{18,26},{... | collective-permute-start | bytes 393224 | tf_op jit(solution)/shard_map/ppermute | solution.py:16
  99.5 1.3 collective-permute-start.13
  100.8 1.2 collective-permute-done.12
  102.0 4.4 %collective-permute-done.13 = f32[1,2,128,128]{3,2,1,0:T(8,128)S(1)} collective-permute-done((f32[1,2,128,128]{3,2,1,0:T(8,128)S(1)}, f32[1,2,128,128]{3,2,1,0:T(8,128)S(1)}, u32[]{:S(2)}, u32[]{:S(2)}) %collective-permute-start.13) | collective-permute-done | bytes 131104 | tf_op jit(solution)/shard_map/ppermute | solution.py:17
  106.3 1.1 fusion.36
  107.5 3.1 %collective-permute-start.14 = (f32[1,2,128,128]{3,2,1,0:T(8,128)S(1)}, f32[1,2,128,128]{3,2,1,0:T(8,128)S(1)}, u32[]{:S(2)}, u32[]{:S(2)}) collective-permute-start(f32[1,2,128,128]{3,2,1,0:T(8,128)S(1)} %get-tuple-element.14), channel_id=1, source_target_pairs={{0,8},{8,16},{16,24},{1,9},{9,17},{17,25},{2,10},{10,18},{18,26},{... | collective-permute-start | bytes 393224 | tf_op jit(solution)/shard_map/ppermute | solution.py:16
  110.6 1.3 collective-permute-start.15
  111.9 1.2 collective-permute-done.14
  113.1 4.4 %collective-permute-done.15 = f32[1,2,128,128]{3,2,1,0:T(8,128)S(1)} collective-permute-done((f32[1,2,128,128]{3,2,1,0:T(8,128)S(1)}, f32[1,2,128,128]{3,2,1,0:T(8,128)S(1)}, u32[]{:S(2)}, u32[]{:S(2)}) %collective-permute-start.15) | collective-permute-done | bytes 131104 | tf_op jit(solution)/shard_map/ppermute | solution.py:17
  117.5 1.2 fusion.33
  119.4 3.5 %collective-permute-start.16 = (f32[1,2,128,128]{3,2,1,0:T(8,128)}, f32[1,2,128,128]{3,2,1,0:T(8,128)}, u32[]{:S(2)}, u32[]{:S(2)}) collective-permute-start(f32[1,2,128,128]{3,2,1,0:T(8,128)} %get-tuple-element.11), channel_id=1, source_target_pairs={{0,8},{8,16},{16,24},{1,9},{9,17},{17,25},{2,10},{10,18},{18,26},{... | collective-permute-start | bytes 393224 | tf_op jit(solution)/shard_map/ppermute | solution.py:16
  122.9 1.3 collective-permute-start.17
  124.8 1.7 reduce_sum.35
  126.6 1.8 reduce_sum.36
  128.4 1.7 reduce_sum.37
  130.1 5.6 %all-gather.11.cloned.1.call-done = f32[8,4,128,128]{3,2,1,0:T(8,128)} async-done(((f32[1,4,128,128]{3,2,1,0:T(8,128)}), f32[8,4,128,128]{3,2,1,0:T(8,128)}) %all-gather.11.cloned.1.call-update) | async-done | bytes 2097168 | tf_op jit(solution)/shard_map/all_gather | solution.py:24
  135.7 2.4 %reduce_sum.41 = f32[4,128,128]{2,1,0:T(8,128)} reduce(f32[8,4,128,128]{3,2,1,0:T(8,128)} %all-gather.11.cloned.1.call-done, f32[]{:T(128)} %constant.77.clone.1), dimensions={0}, to_apply=%region_3.4 | reduce | flops 458752 | bytes 2359300 | tf_op jit(solution)/shard_map/reduce_sum | solution.py:24
  138.1 3.1 %fusion.25 = (f32[4,128,128]{2,1,0:T(8,128)}, f32[1,4,128,128]{3,2,1,0:T(8,128)}) fusion(f32[4,128,128]{2,1,0:T(8,128)} %reduce_sum.41, f32[4,128,128]{2,1,0:T(8,128)S(1)} %reduce_sum.37, f32[4,128,128]{2,1,0:T(8,128)S(1)} %reduce_sum.36, f32[4,128,128]{2,1,0:T(8,128)S(1)} %reduce_sum.35, f32[1,4,128,128]{3,2,1,0:T(8,128)S(1)} %fusion.36, ...), kind=kLoop, calls=%fused_computation.114 | loop fusion | flops 4128768 | bytes 3997724 | tf_op jit(solution)/shard_map/add | solution.py:128
  141.2 30.3 %reduce-scatter.2.cloned.1.call-done = f32[4,16,128]{2,1,0:T(8,128)} async-done(((f32[4,128,128]{2,1,0:T(8,128)}), f32[4,16,128]{2,1,0:T(8,128)}) %reduce-scatter.2.cloned.1.call-update) | async-done | bytes 32784 | tf_op jit(solution)/shard_map/reduce_scatter | solution.py:129
  (46 shorter events, 4.6 us)
Async XLA Ops:
  7.2 7.6 %copy-start = (f32[4,128,128]{2,1,0:T(8,128)S(1)}, f32[4,128,128]{2,1,0:T(8,128)}, u32[]{:S(2)}) copy-start(f32[4,128,128]{2,1,0:T(8,128)} %param.11) | copy-start | bytes 786436
  7.2 7.6 %copy-start.2 = (f32[4,128,128]{2,1,0:T(8,128)S(1)}, f32[4,128,128]{2,1,0:T(8,128)}, u32[]{:S(2)}) copy-start(f32[4,128,128]{2,1,0:T(8,128)} %param.12) | copy-start | bytes 786436
  7.2 117.6 %all-gather.5.cloned.1.call-start = ((), (), s32[]{:S(2)}) async-start(), calls=%async_computation.1 | async-start | bytes 2359296 | tf_op jit(solution)/shard_map/all_gather | solution.py:24
  11.2 9.9 %copy-start.1 = (f32[1,4,128,128]{3,2,1,0:T(8,128)S(1)}, f32[1,4,128,128]{3,2,1,0:T(8,128)}, u32[]{:S(2)}) copy-start(f32[1,4,128,128]{3,2,1,0:T(8,128)} %param.9) | copy-start | bytes 786436
  11.2 16.5 %copy-start.4 = (f32[1,8]{1,0:T(1,128)S(1)}, f32[1,8]{1,0:T(1,128)}, u32[]{:S(2)}) copy-start(f32[1,8]{1,0:T(1,128)} %param.16) | copy-start | bytes 100
  13.3 113.3 %all-gather.7.cloned.1.call-start = ((), (), s32[]{:S(2)}) async-start(), calls=%async_computation.2 | async-start | bytes 2359296 | tf_op jit(solution)/shard_map/all_gather | solution.py:24
  14.0 114.3 %all-gather.9.cloned.1.call-start = ((), (), s32[]{:S(2)}) async-start(), calls=%async_computation.3 | async-start | bytes 2359296 | tf_op jit(solution)/shard_map/all_gather | solution.py:24
  14.8 120.9 %all-gather.11.cloned.1.call-start = ((), (), s32[]{:S(2)}) async-start(), calls=%async_computation.4 | async-start | bytes 2359296 | tf_op jit(solution)/shard_map/all_gather | solution.py:24
  14.9 34.9 %collective-permute-start.2 = (f32[2,4,128,128]{3,2,1,0:T(8,128)S(1)}, f32[2,4,128,128]{3,2,1,0:T(8,128)S(1)}, u32[]{:S(2)}, u32[]{:S(2)}) collective-permute-start(f32[2,4,128,128]{3,2,1,0:T(8,128)S(1)} %pad_maximum_fusion.1), channel_id=1, source_target_pairs={{0,8},{8,16},{16,24},{1,9},{9,17},{17,25},{2,10},{10,18},{18,26},{... | collective-permute-start | bytes 1572872 | tf_op jit(solution)/shard_map/ppermute | solution.py:16
  19.8 30.0 %collective-permute-start.3 = (f32[2,4,128,128]{3,2,1,0:T(8,128)S(1)}, f32[2,4,128,128]{3,2,1,0:T(8,128)S(1)}, u32[]{:S(2)}, u32[]{:S(2)}) collective-permute-start(f32[2,4,128,128]{3,2,1,0:T(8,128)S(1)} %pad_maximum_fusion.1), channel_id=1, source_target_pairs={{8,0},{16,8},{24,16},{9,1},{17,9},{25,17},{10,2},{18,10},{26,18},{... | collective-permute-start | bytes 1572872 | tf_op jit(solution)/shard_map/ppermute | solution.py:17
  21.1 12.6 %collective-permute-start = (f32[1,2,128,128]{3,2,1,0:T(8,128)S(1)}, f32[1,2,128,128]{3,2,1,0:T(8,128)S(1)}, u32[]{:S(2)}, u32[]{:S(2)}) collective-permute-start(f32[1,2,128,128]{3,2,1,0:T(8,128)S(1)} %get-tuple-element.27), channel_id=1, source_target_pairs={{0,8},{8,16},{16,24},{1,9},{9,17},{17,25},{2,10},{10,18},{18,26},{... | collective-permute-start | bytes 393224 | tf_op jit(solution)/shard_map/ppermute | solution.py:16
  25.7 24.0 %collective-permute-start.1 = (f32[1,2,128,128]{3,2,1,0:T(8,128)S(1)}, f32[1,2,128,128]{3,2,1,0:T(8,128)S(1)}, u32[]{:S(2)}, u32[]{:S(2)}) collective-permute-start(f32[1,2,128,128]{3,2,1,0:T(8,128)S(1)} %get-tuple-element.28), channel_id=1, source_target_pairs={{8,0},{16,8},{24,16},{9,1},{17,9},{25,17},{10,2},{18,10},{26,18},{... | collective-permute-start | bytes 393224 | tf_op jit(solution)/shard_map/ppermute | solution.py:17
  50.0 1.0 copy-start.3
  52.3 5.9 %collective-permute-start.4 = (f32[1,2,128,128]{3,2,1,0:T(8,128)S(1)}, f32[1,2,128,128]{3,2,1,0:T(8,128)S(1)}, u32[]{:S(2)}, u32[]{:S(2)}) collective-permute-start(f32[1,2,128,128]{3,2,1,0:T(8,128)S(1)} %get-tuple-element.24), channel_id=1, source_target_pairs={{0,8},{8,16},{16,24},{1,9},{9,17},{17,25},{2,10},{10,18},{18,26},{... | collective-permute-start | bytes 393224 | tf_op jit(solution)/shard_map/ppermute | solution.py:16
  55.7 6.9 %collective-permute-start.5 = (f32[1,2,128,128]{3,2,1,0:T(8,128)S(1)}, f32[1,2,128,128]{3,2,1,0:T(8,128)S(1)}, u32[]{:S(2)}, u32[]{:S(2)}) collective-permute-start(f32[1,2,128,128]{3,2,1,0:T(8,128)S(1)} %get-tuple-element.23), channel_id=1, source_target_pairs={{8,0},{16,8},{24,16},{9,1},{17,9},{25,17},{10,2},{18,10},{26,18},{... | collective-permute-start | bytes 393224 | tf_op jit(solution)/shard_map/ppermute | solution.py:17
  57.0 114.5 %reduce-scatter.2.cloned.1.call-start = ((), (), s32[]{:S(2)}) async-start(), calls=%async_computation.5 | async-start | bytes 294912 | tf_op jit(solution)/shard_map/reduce_scatter | solution.py:129
  63.7 5.3 %collective-permute-start.6 = (f32[1,2,128,128]{3,2,1,0:T(8,128)S(1)}, f32[1,2,128,128]{3,2,1,0:T(8,128)S(1)}, u32[]{:S(2)}, u32[]{:S(2)}) collective-permute-start(f32[1,2,128,128]{3,2,1,0:T(8,128)S(1)} %get-tuple-element.22), channel_id=1, source_target_pairs={{0,8},{8,16},{16,24},{1,9},{9,17},{17,25},{2,10},{10,18},{18,26},{... | collective-permute-start | bytes 393224 | tf_op jit(solution)/shard_map/ppermute | solution.py:16
  66.5 6.9 %collective-permute-start.7 = (f32[1,2,128,128]{3,2,1,0:T(8,128)S(1)}, f32[1,2,128,128]{3,2,1,0:T(8,128)S(1)}, u32[]{:S(2)}, u32[]{:S(2)}) collective-permute-start(f32[1,2,128,128]{3,2,1,0:T(8,128)S(1)} %get-tuple-element.21), channel_id=1, source_target_pairs={{8,0},{16,8},{24,16},{9,1},{17,9},{25,17},{10,2},{18,10},{26,18},{... | collective-permute-start | bytes 393224 | tf_op jit(solution)/shard_map/ppermute | solution.py:17
  74.6 5.3 %collective-permute-start.8 = (f32[1,2,128,128]{3,2,1,0:T(8,128)S(1)}, f32[1,2,128,128]{3,2,1,0:T(8,128)S(1)}, u32[]{:S(2)}, u32[]{:S(2)}) collective-permute-start(f32[1,2,128,128]{3,2,1,0:T(8,128)S(1)} %get-tuple-element.20), channel_id=1, source_target_pairs={{0,8},{8,16},{16,24},{1,9},{9,17},{17,25},{2,10},{10,18},{18,26},{... | collective-permute-start | bytes 393224 | tf_op jit(solution)/shard_map/ppermute | solution.py:16
  77.5 6.9 %collective-permute-start.9 = (f32[1,2,128,128]{3,2,1,0:T(8,128)S(1)}, f32[1,2,128,128]{3,2,1,0:T(8,128)S(1)}, u32[]{:S(2)}, u32[]{:S(2)}) collective-permute-start(f32[1,2,128,128]{3,2,1,0:T(8,128)S(1)} %get-tuple-element.19), channel_id=1, source_target_pairs={{8,0},{16,8},{24,16},{9,1},{17,9},{25,17},{10,2},{18,10},{26,18},{... | collective-permute-start | bytes 393224 | tf_op jit(solution)/shard_map/ppermute | solution.py:17
  85.5 5.3 %collective-permute-start.10 = (f32[1,2,128,128]{3,2,1,0:T(8,128)S(1)}, f32[1,2,128,128]{3,2,1,0:T(8,128)S(1)}, u32[]{:S(2)}, u32[]{:S(2)}) collective-permute-start(f32[1,2,128,128]{3,2,1,0:T(8,128)S(1)} %get-tuple-element.18), channel_id=1, source_target_pairs={{0,8},{8,16},{16,24},{1,9},{9,17},{17,25},{2,10},{10,18},{18,26},{... | collective-permute-start | bytes 393224 | tf_op jit(solution)/shard_map/ppermute | solution.py:16
  88.3 6.9 %collective-permute-start.11 = (f32[1,2,128,128]{3,2,1,0:T(8,128)S(1)}, f32[1,2,128,128]{3,2,1,0:T(8,128)S(1)}, u32[]{:S(2)}, u32[]{:S(2)}) collective-permute-start(f32[1,2,128,128]{3,2,1,0:T(8,128)S(1)} %get-tuple-element.17), channel_id=1, source_target_pairs={{8,0},{16,8},{24,16},{9,1},{17,9},{25,17},{10,2},{18,10},{26,18},{... | collective-permute-start | bytes 393224 | tf_op jit(solution)/shard_map/ppermute | solution.py:17
  96.4 5.6 %collective-permute-start.12 = (f32[1,2,128,128]{3,2,1,0:T(8,128)S(1)}, f32[1,2,128,128]{3,2,1,0:T(8,128)S(1)}, u32[]{:S(2)}, u32[]{:S(2)}) collective-permute-start(f32[1,2,128,128]{3,2,1,0:T(8,128)S(1)} %get-tuple-element.16), channel_id=1, source_target_pairs={{0,8},{8,16},{16,24},{1,9},{9,17},{17,25},{2,10},{10,18},{18,26},{... | collective-permute-start | bytes 393224 | tf_op jit(solution)/shard_map/ppermute | solution.py:16
  99.5 6.9 %collective-permute-start.13 = (f32[1,2,128,128]{3,2,1,0:T(8,128)S(1)}, f32[1,2,128,128]{3,2,1,0:T(8,128)S(1)}, u32[]{:S(2)}, u32[]{:S(2)}) collective-permute-start(f32[1,2,128,128]{3,2,1,0:T(8,128)S(1)} %get-tuple-element.15), channel_id=1, source_target_pairs={{8,0},{16,8},{24,16},{9,1},{17,9},{25,17},{10,2},{18,10},{26,18},{... | collective-permute-start | bytes 393224 | tf_op jit(solution)/shard_map/ppermute | solution.py:17
  107.5 5.7 %collective-permute-start.14 = (f32[1,2,128,128]{3,2,1,0:T(8,128)S(1)}, f32[1,2,128,128]{3,2,1,0:T(8,128)S(1)}, u32[]{:S(2)}, u32[]{:S(2)}) collective-permute-start(f32[1,2,128,128]{3,2,1,0:T(8,128)S(1)} %get-tuple-element.14), channel_id=1, source_target_pairs={{0,8},{8,16},{16,24},{1,9},{9,17},{17,25},{2,10},{10,18},{18,26},{... | collective-permute-start | bytes 393224 | tf_op jit(solution)/shard_map/ppermute | solution.py:16
  110.6 6.9 %collective-permute-start.15 = (f32[1,2,128,128]{3,2,1,0:T(8,128)S(1)}, f32[1,2,128,128]{3,2,1,0:T(8,128)S(1)}, u32[]{:S(2)}, u32[]{:S(2)}) collective-permute-start(f32[1,2,128,128]{3,2,1,0:T(8,128)S(1)} %get-tuple-element.13), channel_id=1, source_target_pairs={{8,0},{16,8},{24,16},{9,1},{17,9},{25,17},{10,2},{18,10},{26,18},{... | collective-permute-start | bytes 393224 | tf_op jit(solution)/shard_map/ppermute | solution.py:17
  119.4 18.7 %collective-permute-start.16 = (f32[1,2,128,128]{3,2,1,0:T(8,128)}, f32[1,2,128,128]{3,2,1,0:T(8,128)}, u32[]{:S(2)}, u32[]{:S(2)}) collective-permute-start(f32[1,2,128,128]{3,2,1,0:T(8,128)} %get-tuple-element.11), channel_id=1, source_target_pairs={{0,8},{8,16},{16,24},{1,9},{9,17},{17,25},{2,10},{10,18},{18,26},{... | collective-permute-start | bytes 393224 | tf_op jit(solution)/shard_map/ppermute | solution.py:16
  122.9 15.3 %collective-permute-start.17 = (f32[1,2,128,128]{3,2,1,0:T(8,128)}, f32[1,2,128,128]{3,2,1,0:T(8,128)}, u32[]{:S(2)}, u32[]{:S(2)}) collective-permute-start(f32[1,2,128,128]{3,2,1,0:T(8,128)} %get-tuple-element.12), channel_id=1, source_target_pairs={{8,0},{16,8},{24,16},{9,1},{17,9},{25,17},{10,2},{18,10},{26,18},{... | collective-permute-start | bytes 393224 | tf_op jit(solution)/shard_map/ppermute | solution.py:17
Sparse Core Ops, SparseCore 0:
  13.4 31.8 all-gather.4
  46.9 28.5 all-gather.6
  77.1 28.5 all-gather.8
  107.1 28.5 all-gather.10
  141.3 30.1 reduce-scatter.1
